TPU v7x, 256 devices: a whole 4x4x8 slice. The times are simulated.
256 devices in a mesh: tm: 32 (over y, z), space: 8 (over x, core).
Axes of the slice: x: 4, y: 4, z: 8, core: 2. Of those that a mesh axis runs over, the one named last changes fastest.
Arguments:
- inverse_factor: bfloat16 [2, 32, 4096, 4096], P(None, 'tm', 'space'), may hold values from -1.5 to 1.5, as said below
- tile_mask: int32 [32, 32], replicated, may hold values 0 or 1
- carry_rate: float32 [32, 4096, 2], P('tm', 'space'), may hold values from 0 to 1
- right_side: float32 [32, 4096, 2, 128], P('tm', 'space'), may hold values from -1.5 to 1.5
- arrow_rows: bfloat16 [32, 4096, 2, 512], P('tm', 'space'), may hold values from -0.0625 to 0.0625
- fixed_rhs: float32 [2, 512, 128], P(None, ('tm', 'space')), may hold values from -6 to 6
- tip_factor: bfloat16 [2, 512, 512], replicated, may hold values from -1 to 1, as said below
Outputs:
- solution: float32 [32, 4096, 2, 128], P('tm', 'space')
- fixed_solution: float32 [2, 512, 128], P(None, ('tm', 'space'))
Inputs may be any that keep to these rules, and one draw needn't show every extreme that they name: `tile_mask`: 1 marks a tile that may be nonzero. `inverse_factor`: only entries on or below the diagonal are read. `tip_factor`: only entries on or below the diagonal are read.
All inputs are finite; a program needn't handle non-finite values.
Results may differ from a plain program's by a relative error of at most 0.022.
Values may be sent and summed in bfloat16 or wider, within the bound.
No kernel may reach another device: no remote copies, remote signals or barrier semaphores. Data moves between devices by JAX's collectives and lax.ppermute only.
A program may use at most 320 MiB of HBM per device.

v0:
```python
import jax
import jax.numpy as jnp
from jax import lax
from jax.sharding import PartitionSpec as P

TILE = 128


def carried_in(shard, axis, join, neutral, backward):
    count = lax.axis_size(axis)
    place = lax.axis_index(axis)
    ahead = count - 1 - place if backward else place
    gathered = jax.tree.map(
        lambda a, kind: lax.all_gather(a.astype(kind), axis), shard, (jnp.bfloat16, jnp.bfloat16)
    )
    state = jax.tree.map(lambda a, e: jnp.zeros_like(a) + jnp.asarray(e, a.dtype), shard, neutral)

    def one(turn, state):
        source = count - 1 - turn if backward else turn
        return join(
            state,
            jax.tree.map(
                lambda a, own: lax.dynamic_index_in_dim(a, source, 0, False).astype(own.dtype),
                gathered,
                shard,
            ),
        )

    return lax.fori_loop(0, ahead, one, state)


def combine(earlier, latter):
    rate_new = latter[0] * earlier[0]
    rest = tuple(
        (value_l + latter[0] * value_e for value_l, value_e in zip(latter[1:], earlier[1:]))
    )
    return (rate_new,) + rest


def tile_keep(tile_table, row_start, row_total, col_total):
    tile_count = tile_table.shape[0]
    tile_ids = jnp.arange(tile_count, dtype=jnp.int32)
    row_index = row_start + jnp.arange(row_total, dtype=jnp.int32)
    col_index = jnp.arange(col_total, dtype=jnp.int32)
    row_onehot = (row_index[:, None] // TILE == tile_ids[None, :]).astype(jnp.float32)
    col_onehot = (col_index[:, None] // TILE == tile_ids[None, :]).astype(jnp.float32)
    marked = jnp.dot(jnp.dot(row_onehot, tile_table.astype(jnp.float32)), col_onehot.T)
    return (marked > 0.5) & (row_index[:, None] >= col_index[None, :])


def on_device(inverse_factor, tile_mask, carry_rate, right_side, arrow_rows, fixed_rhs, tip_factor):
    row_count = right_side.shape[1]
    node_total = inverse_factor.shape[3]
    row_start = lax.axis_index("space") * row_count
    tile_table = jnp.maximum(tile_mask, jnp.eye(tile_mask.shape[0], dtype=jnp.int32))
    weights = inverse_factor[:, 0]
    bf_zero = jnp.zeros((), jnp.bfloat16)
    rate_col = carry_rate[0][:, :, None]
    source = right_side[0]
    unit_rate = jnp.ones_like(rate_col)
    earlier_sum = carried_in(
        (rate_col, source), "tm", combine, (unit_rate, jnp.zeros_like(source)), False
    )
    forward = source + rate_col * earlier_sum[1]
    forward_b = forward.astype(jnp.bfloat16)
    row_keep = tile_keep(tile_table, row_start, row_count, node_total)
    masked_rows = jnp.where(row_keep[None], weights, bf_zero)
    block = masked_rows
    inner_rows = jnp.einsum(
        "hrn,nhk->rhk",
        block,
        lax.all_gather(forward_b, "space", axis=0, tiled=True),
        preferred_element_type=jnp.float32,
    ).astype(jnp.bfloat16)
    block = masked_rows
    scaled = lax.psum_scatter(
        jnp.einsum("hrn,rhk->nhk", block, inner_rows, preferred_element_type=jnp.float32).astype(
            jnp.bfloat16
        ),
        "space",
        scatter_dimension=0,
        tiled=True,
    ).astype(jnp.float32)
    arrow_part = arrow_rows[0]
    coupling = jnp.einsum("rhf,rhk->hfk", arrow_part, forward_b, preferred_element_type=jnp.float32)
    share_rows = fixed_rhs.shape[1]
    share_start = lax.axis_index(("tm", "space")) * share_rows
    contrib = -coupling
    own_part = lax.dynamic_slice_in_dim(contrib, share_start, share_rows, 1) + fixed_rhs
    contrib = lax.dynamic_update_slice_in_dim(contrib, own_part, share_start, 1)
    fixed_forward = lax.psum(contrib, ("tm", "space")).astype(jnp.bfloat16)
    fixed_total = tip_factor.shape[1]
    fixed_index = jnp.arange(fixed_total, dtype=jnp.int32)
    lower_tri = fixed_index[:, None] >= fixed_index[None, :]
    tip_lower = jnp.where(lower_tri[None], tip_factor, bf_zero)
    tip_inner = jnp.einsum(
        "hij,hjk->hik", tip_lower, fixed_forward, preferred_element_type=jnp.float32
    ).astype(jnp.bfloat16)
    fixed_solution = jnp.einsum(
        "hij,hik->hjk", tip_lower, tip_inner, preferred_element_type=jnp.float32
    )
    fixed_own = lax.dynamic_slice_in_dim(fixed_solution, share_start, share_rows, 1)
    fixed_b = fixed_solution.astype(jnp.bfloat16)
    carried = scaled - jnp.einsum(
        "rhf,hfk->rhk", arrow_part, fixed_b, preferred_element_type=jnp.float32
    )
    following = carried_in(
        (rate_col, rate_col * carried), "tm", combine, (unit_rate, jnp.zeros_like(carried)), True
    )
    solution = carried + following[1]
    return (solution[None], fixed_own)


def solution(mesh):
    placed = (
        P(None, "tm", "space", None),
        P(),
        P("tm", "space", None),
        P("tm", "space", None, None),
        P("tm", "space", None, None),
        P(None, ("tm", "space"), None),
        P(),
    )
    return jax.shard_map(
        on_device,
        mesh=mesh,
        in_specs=placed,
        out_specs=(P("tm", "space", None, None), P(None, ("tm", "space"), None)),
        check_vma=False,
    )
```

profile of v0, /device:TPU:2, one launch (start us, length us, event | category | flops | bytes accessed | tf_op | source)
XLA Modules:
  0.0 596.0 jit_solution(12626880782622736189)
XLA Ops:
  11.1 52.1 %all-gather = bf16[32,512,2]{1,2,0:T(2,128)(2,1)S(1)} all-gather(bf16[1,512,2]{1,2,0:T(2,128)(2,1)S(1)} %convert_element_type.103), channel_id=2, replica_groups=mesh['tm'=32,'space'=8] {'tm'}, dimensions={0}, use_global_device_ids=true | all-gather | bytes 67584 | tf_op jit(solution)/shard_map/all_gather | solution.py:14
  63.2 3.3 copy.37
  66.6 46.1 %all-gather.6.cloned.1.call-done = bf16[32,512,2,128]{3,1,2,0:T(8,128)(2,1)} async-done(((bf16[1,512,2,128]{3,1,2,0:T(8,128)(2,1)}), bf16[32,512,2,128]{3,1,2,0:T(8,128)(2,1)}) %all-gather.6.cloned.1.call-update) | async-done | bytes 8388624 | tf_op jit(solution)/shard_map/all_gather | solution.py:14
  114.4 4.2 fusion
  118.6 154.2 %all-gather.8.cloned.1.call-done = bf16[4096,2,128]{0,2,1:T(8,128)(2,1)} async-done(((bf16[512,2,128]{0,2,1:T(8,128)(2,1)}), bf16[4096,2,128]{0,2,1:T(8,128)(2,1)}) %all-gather.8.cloned.1.call-update) | async-done | bytes 2097168 | tf_op jit(solution)/shard_map/all_gather | solution.py:72
  272.7 13.2 %fusion.4 = bf16[4096,2,128]{0,2,1:T(8,128)(2,1)} fusion(bf16[2,1,512,4096]{3,2,1,0:T(8,128)(2,1)} %param.11, pred[512,4096]{1,0:T(8,128)(4,1)} %fusion, bf16[4096,2,128]{0,2,1:T(8,128)(2,1)} %all-gather.8.cloned.1.call-done), kind=kOutput, calls=%fused_computation.12 | convolution fusion | flops 2157051904 | bytes 14680064 | tf_op jit(solution)/shard_map/hrn,rhk->nhk/dot_general | solution.py:77
  287.8 78.9 %all-reduce.1 = bf16[2,512,128]{1,2,0:T(8,128)(2,1)S(1)} all-reduce(f32[2,512,128]{1,2,0:T(8,128)S(1)} %dynamic_update_slice.3), channel_id=1, replica_groups=mesh['tm'=32,'space'=8] {'tm','space'}, use_global_device_ids=true, to_apply=%region_3.4 | all-reduce | flops 131072 | bytes 786432 | tf_op jit(solution)/shard_map/psum | solution.py:91
  366.7 2.3 fusion.9
  369.0 2.1 multiply_convert_fusion
  371.8 102.9 %all-gather.10.cloned.1.call-done = bf16[16384,2,128]{0,2,1:T(8,128)(2,1)} async-done(((bf16[512,2,128]{0,2,1:T(8,128)(2,1)}), bf16[16384,2,128]{0,2,1:T(8,128)(2,1)}) %all-gather.10.cloned.1.call-update) | async-done | bytes 8388624 | tf_op jit(solution)/shard_map/all_gather | solution.py:14
  474.7 21.1 %copy.52 = bf16[16384,2,128]{2,1,0:T(2,128)(2,1)} copy(bf16[16384,2,128]{0,2,1:T(8,128)(2,1)} %all-gather.10.cloned.1.call-done) | data formatting | bytes 16777216 | tf_op jit(solution)/shard_map/while | solution.py:29
  495.9 92.2 %while.27 = (s32[]{:T(128)}, f32[512,2,128]{2,1,0:T(2,128)S(1)}, s32[]{:T(128)}, bf16[32,512,2,128]{3,2,1,0:T(2,128)(2,1)}, bf16[32,512,2,1]{2,1,3,0:T(8,128)(2,...) while((s32[]{:T(128)}, f32[512,2,128]{2,1,0:T(2,128)S(1)}, s32[]{:T(128)}, ...), condition=%wide.region_5.6_spmd, body=%wide.region_4.5_spmd.sunk | while | flops 394246 | bytes 1321107 | solution.py:29
  499.8 2.0 convert_add_fusion.5
  502.8 2.0 convert_add_fusion.5
  505.8 2.0 convert_add_fusion.5
  508.8 2.0 convert_add_fusion.5
  511.7 2.0 convert_add_fusion.5
  520.7 2.0 convert_add_fusion.5
  523.6 2.0 convert_add_fusion.5
  526.6 2.0 convert_add_fusion.5
  529.6 2.0 convert_add_fusion.5
  538.5 2.0 convert_add_fusion.5
  541.5 2.0 convert_add_fusion.5
  544.5 2.0 convert_add_fusion.5
  547.4 2.0 convert_add_fusion.5
  556.3 2.0 convert_add_fusion.5
  559.3 2.0 convert_add_fusion.5
  562.3 2.0 convert_add_fusion.5
  565.3 2.0 convert_add_fusion.5
  568.2 2.0 convert_add_fusion.5
  577.2 2.0 convert_add_fusion.5
  580.1 2.0 convert_add_fusion.5
  (80 shorter events, 60.3 us)
Async XLA Ops:
  7.2 279.1 %copy-start = (bf16[1,512,2,512]{3,2,1,0:T(2,128)(2,1)S(1)}, bf16[1,512,2,512]{3,2,1,0:T(2,128)(2,1)}, u32[]{:S(2)}) copy-start(bf16[1,512,2,512]{3,2,1,0:T(2,128)(2,1)} %param.15) | copy-start | bytes 3145732
  7.2 105.5 %all-gather.6.cloned.1.call-start = ((), (), s32[]{:S(2)}) async-start(), calls=%async_computation.1 | async-start | bytes 8650752 | tf_op jit(solution)/shard_map/all_gather | solution.py:14
  9.1 263.6 %all-gather.8.cloned.1.call-start = ((), (), s32[]{:S(2)}) async-start(), calls=%async_computation.2 | async-start | bytes 2359296 | tf_op jit(solution)/shard_map/all_gather | solution.py:72
  112.8 0.7 copy-start.2
  112.8 1.6 copy-start.4
  114.3 254.7 %reduce-scatter.2.cloned.1.call-start = ((), (), s32[]{:S(2)}) async-start(), calls=%async_computation.3 | async-start | bytes 2359296 | tf_op jit(solution)/shard_map/reduce_scatter | solution.py:76
  118.6 167.5 %copy-start.3 = (f32[2,2,128]{2,1,0:T(2,128)S(1)}, f32[2,2,128]{2,1,0:T(2,128)}, u32[]{:S(2)}) copy-start(f32[2,2,128]{2,1,0:T(2,128)} %param.16) | copy-start | bytes 6148
  118.6 167.7 %copy-start.1 = (bf16[512,2,128]{0,2,1:T(8,128)(2,1)S(1)}, bf16[512,2,128]{0,2,1:T(8,128)(2,1)}, u32[]{:S(2)}) copy-start(bf16[512,2,128]{0,2,1:T(8,128)(2,1)} %fusion.19) | copy-start | bytes 786436
  286.0 188.7 %all-gather.10.cloned.1.call-start = ((), (), s32[]{:S(2)}) async-start(), calls=%async_computation.4 | async-start | bytes 8650752 | tf_op jit(solution)/shard_map/all_gather | solution.py:14
Sparse Core Ops, SparseCore 0:
  11.2 101.4 all-gather.5
  115.0 157.6 all-gather.7
  286.1 34.6 reduce-scatter.1
  371.3 103.2 all-gather.9
where the time goes:
time: 598 us; the launch traced here: 596 us
  waiting for transfers between devices  303 us (51%)
  blocking collectives  131 us (22%)
  other arithmetic  92.9 us (16%)
  local copies, waits for them, and re-layouts  31.4 us (5%)
  matrix products  22.2 us (4%)
  between operations  14 us (2%)
    all_gather x1, waiting for transfers between devices, on_device(): lax.all_gather(forward_b, 'space', axis=0, tiled=True)  154 us
    all_gather x2, waiting for transfers between devices, carried_in(): lax.all_gather(a.astype(kind), axis)  149 us
    psum x1, blocking collectives, on_device(): fixed_forward = lax.psum(contrib, ('tm', 'space')).astype(jnp.bfloat16)  78.9 us
    add x31, other arithmetic, combine(): value_l + latter[0] * value_e  62.3 us
    all_gather x1, blocking collectives, carried_in(): lax.all_gather(a.astype(kind), axis)  52.1 us
    convert_element_type x31, other arithmetic, one(): lax.dynamic_index_in_dim(a, source, 0, False).astype(own.dtype)  28.8 us
    while x4, local copies, waits for them, and re-layouts, carried_in(): return lax.fori_loop(0, ahead, one, state)  24.8 us
    dot_general x1, matrix products, on_device(): jnp.einsum('hrn,rhk->nhk', block, inner_rows, preferred_element_type=jnp....  13.2 us
  transfers between devices with their start and end apart: 4, of which 3 were waited for; matrix products, arithmetic and copies ran while one was open for 2% of the time, Pallas kernels for 0%

commit v1 on v0

--- a/solution.py
+++ b/solution.py
@@ -88,7 +88,7 @@
     contrib = -coupling
     own_part = lax.dynamic_slice_in_dim(contrib, share_start, share_rows, 1) + fixed_rhs
     contrib = lax.dynamic_update_slice_in_dim(contrib, own_part, share_start, 1)
-    fixed_forward = lax.psum(contrib, ("tm", "space")).astype(jnp.bfloat16)
+    fixed_forward = lax.psum(lax.psum(contrib, "space"), "tm").astype(jnp.bfloat16)
     fixed_total = tip_factor.shape[1]
     fixed_index = jnp.arange(fixed_total, dtype=jnp.int32)
     lower_tri = fixed_index[:, None] >= fixed_index[None, :]

time: 598 us -> 715 us (1.20)
  blocking collectives: 131 us -> 200 us
  waiting for transfers between devices: 303 us -> 350 us
    psum x1, blocking collectives: 78.9 us -> 148 us  [on_device(): lax.psum(lax.psum(contrib, 'space'), 'tm').astype(jnp.bfloat16)]
    psum x0 -> x1, waiting for transfers between devices: none -> 54.2 us  [on_device(): lax.psum(contrib, 'space')]
  transfers between devices with their start and end apart: 4 -> 5, of which waited for: 3 -> 4; matrix products, arithmetic and copies ran while one was open for 2% -> 4% of each run, Pallas kernels for 0% -> 0%
where the time goes in v1:
time: 715 us; the launch traced here: 713 us
  waiting for transfers between devices  350 us (49%)
  blocking collectives  200 us (28%)
  other arithmetic  92.9 us (13%)
  local copies, waits for them, and re-layouts  32.3 us (5%)
  matrix products  22.3 us (3%)
  between operations  14 us (2%)
    all_gather x1, waiting for transfers between devices, on_device(): lax.all_gather(forward_b, 'space', axis=0, tiled=True)  152 us
    psum x1, blocking collectives, on_device(): lax.psum(lax.psum(contrib, 'space'), 'tm').astype(jnp.bfloat16)  148 us
    all_gather x2, waiting for transfers between devices, carried_in(): lax.all_gather(a.astype(kind), axis)  144 us
    add x31, other arithmetic, combine(): value_l + latter[0] * value_e  62.3 us
    psum x1, waiting for transfers between devices, on_device(): lax.psum(contrib, 'space')  54.2 us
    all_gather x1, blocking collectives, carried_in(): lax.all_gather(a.astype(kind), axis)  52.1 us
    convert_element_type x31, other arithmetic, one(): lax.dynamic_index_in_dim(a, source, 0, False).astype(own.dtype)  28.8 us
    while x4, local copies, waits for them, and re-layouts, carried_in(): return lax.fori_loop(0, ahead, one, state)  24.9 us
  transfers between devices with their start and end apart: 5, of which 4 were waited for; matrix products, arithmetic and copies ran while one was open for 4% of the time, Pallas kernels for 0%

profile of v1, /device:TPU:2, one launch (start us, length us, event | category | flops | bytes accessed | tf_op | source)
XLA Modules:
  0.0 712.8 jit_solution(9388366884239099188)
XLA Ops:
  11.1 52.1 %all-gather = bf16[32,512,2]{1,2,0:T(2,128)(2,1)S(1)} all-gather(bf16[1,512,2]{1,2,0:T(2,128)(2,1)S(1)} %convert_element_type.103), channel_id=2, replica_groups=mesh['tm'=32,'space'=8] {'tm'}, dimensions={0}, use_global_device_ids=true | all-gather | bytes 67584 | tf_op jit(solution)/shard_map/all_gather | solution.py:14
  63.2 3.3 copy.37
  66.6 46.1 %all-gather.6.cloned.1.call-done = bf16[32,512,2,128]{3,1,2,0:T(8,128)(2,1)} async-done(((bf16[1,512,2,128]{3,1,2,0:T(8,128)(2,1)}), bf16[32,512,2,128]{3,1,2,0:T(8,128)(2,1)}) %all-gather.6.cloned.1.call-update) | async-done | bytes 8388624 | tf_op jit(solution)/shard_map/all_gather | solution.py:14
  114.6 4.2 fusion
  121.1 151.6 %all-gather.8.cloned.1.call-done = bf16[4096,2,128]{0,2,1:T(8,128)(2,1)} async-done(((bf16[512,2,128]{0,2,1:T(8,128)(2,1)}), bf16[4096,2,128]{0,2,1:T(8,128)(2,1)}) %all-gather.8.cloned.1.call-update) | async-done | bytes 2097168 | tf_op jit(solution)/shard_map/all_gather | solution.py:72
  272.7 13.4 %fusion.4 = bf16[4096,2,128]{0,2,1:T(8,128)(2,1)} fusion(bf16[2,1,512,4096]{3,2,1,0:T(8,128)(2,1)} %param.11, pred[512,4096]{1,0:T(8,128)(4,1)} %fusion, bf16[4096,2,128]{0,2,1:T(8,128)(2,1)} %all-gather.8.cloned.1.call-done), kind=kOutput, calls=%fused_computation.12 | convolution fusion | flops 2157051904 | bytes 14680064 | tf_op jit(solution)/shard_map/hrn,rhk->nhk/dot_general | solution.py:77
  286.3 54.2 %all-reduce.3.cloned.1.call-done = f32[2,512,128]{1,2,0:T(8,128)} async-done(((f32[2,512,128]{1,2,0:T(8,128)}), f32[2,512,128]{1,2,0:T(8,128)}) %all-reduce.3.cloned.1.call-update) | async-done | bytes 524304 | tf_op jit(solution)/shard_map/psum | solution.py:91
  340.5 148.3 %all-reduce.4 = bf16[2,512,128]{1,2,0:T(8,128)(2,1)S(1)} all-reduce(f32[2,512,128]{1,2,0:T(8,128)} %all-reduce.3.cloned.1.call-done), channel_id=1, replica_groups=mesh['tm'=32,'space'=8] {'tm'}, use_global_device_ids=true, to_apply=%region_4.5 | all-reduce | flops 131072 | bytes 786432 | tf_op jit(solution)/shard_map/psum | solution.py:91
  488.8 2.3 fusion.9
  491.2 2.1 multiply_convert_fusion
  494.0 97.6 %all-gather.10.cloned.1.call-done = bf16[16384,2,128]{0,2,1:T(8,128)(2,1)} async-done(((bf16[512,2,128]{0,2,1:T(8,128)(2,1)}), bf16[16384,2,128]{0,2,1:T(8,128)(2,1)}) %all-gather.10.cloned.1.call-update) | async-done | bytes 8388624 | tf_op jit(solution)/shard_map/all_gather | solution.py:14
  591.5 21.1 %copy.52 = bf16[16384,2,128]{2,1,0:T(2,128)(2,1)} copy(bf16[16384,2,128]{0,2,1:T(8,128)(2,1)} %all-gather.10.cloned.1.call-done) | data formatting | bytes 16777216 | tf_op jit(solution)/shard_map/while | solution.py:29
  612.8 92.2 %while.27 = (s32[]{:T(128)}, f32[512,2,128]{2,1,0:T(2,128)S(1)}, s32[]{:T(128)}, bf16[32,512,2,128]{3,2,1,0:T(2,128)(2,1)}, bf16[32,512,2,1]{2,1,3,0:T(8,128)(2,...) while((s32[]{:T(128)}, f32[512,2,128]{2,1,0:T(2,128)S(1)}, s32[]{:T(128)}, ...), condition=%wide.region_6.7_spmd, body=%wide.region_5.6_spmd.sunk | while | flops 394246 | bytes 1321107 | solution.py:29
  613.7 2.0 convert_add_fusion.5
  616.7 2.0 convert_add_fusion.5
  619.7 2.0 convert_add_fusion.5
  622.6 2.0 convert_add_fusion.5
  631.6 2.0 convert_add_fusion.5
  634.5 2.0 convert_add_fusion.5
  637.5 2.0 convert_add_fusion.5
  640.5 2.0 convert_add_fusion.5
  643.5 2.0 convert_add_fusion.5
  652.4 2.0 convert_add_fusion.5
  655.4 2.0 convert_add_fusion.5
  658.3 2.0 convert_add_fusion.5
  661.3 2.0 convert_add_fusion.5
  670.2 2.0 convert_add_fusion.5
  673.2 2.0 convert_add_fusion.5
  676.2 2.0 convert_add_fusion.5
  679.2 2.0 convert_add_fusion.5
  688.1 2.0 convert_add_fusion.5
  691.1 2.0 convert_add_fusion.5
  (85 shorter events, 63.2 us)
Async XLA Ops:
  7.2 111.6 %copy-start = (bf16[1,512,2,512]{3,2,1,0:T(2,128)(2,1)S(1)}, bf16[1,512,2,512]{3,2,1,0:T(2,128)(2,1)}, u32[]{:S(2)}) copy-start(bf16[1,512,2,512]{3,2,1,0:T(2,128)(2,1)} %param.15) | copy-start | bytes 3145732
  7.2 105.5 %all-gather.6.cloned.1.call-start = ((), (), s32[]{:S(2)}) async-start(), calls=%async_computation.1 | async-start | bytes 8650752 | tf_op jit(solution)/shard_map/all_gather | solution.py:14
  9.1 263.6 %all-gather.8.cloned.1.call-start = ((), (), s32[]{:S(2)}) async-start(), calls=%async_computation.2 | async-start | bytes 2359296 | tf_op jit(solution)/shard_map/all_gather | solution.py:72
  112.8 0.7 copy-start.3
  112.8 1.6 copy-start.4
  112.8 1.7 copy-start.5
  114.3 226.2 %all-reduce.3.cloned.1.call-start = ((), (), s32[]{:S(2)}) async-start(), calls=%async_computation.4 | async-start | bytes 1048576 | tf_op jit(solution)/shard_map/psum | solution.py:91
  114.5 4.2 copy-start.2
  120.2 0.8 copy-start.1
  121.1 370.1 %reduce-scatter.2.cloned.1.call-start = ((), (), s32[]{:S(2)}) async-start(), calls=%async_computation.3 | async-start | bytes 2359296 | tf_op jit(solution)/shard_map/reduce_scatter | solution.py:76
  286.1 305.4 %all-gather.10.cloned.1.call-start = ((), (), s32[]{:S(2)}) async-start(), calls=%async_computation.5 | async-start | bytes 8650752 | tf_op jit(solution)/shard_map/all_gather | solution.py:14
Sparse Core Ops, SparseCore 0:
  11.2 101.4 all-gather.5
  114.5 158.2 all-gather.7
  275.7 64.8 all-reduce.2
  343.1 34.5 reduce-scatter.1
  493.5 97.9 all-gather.9
